TPU v7x, 512 devices: a whole 4x8x8 slice. The times are simulated.
512 devices in a mesh: opt: 128 (over y, z, core), layer: 4 (over x).
Axes of the slice: x: 4, y: 8, z: 8, core: 2. Of those that a mesh axis runs over, the one named last changes fastest.
Arguments:
- momentum: bfloat16 [4, 128, 1024, 512], P('layer', None, 'opt'), may hold values from -4000 to 4000
- weights: bfloat16 [4, 128, 1024, 512], P('layer', None, 'opt'), may hold values from -6 to 6
Outputs:
- new_weights: bfloat16 [4, 128, 1024, 512], P('layer', None, 'opt')
All inputs are finite; a program needn't handle non-finite values.
Results may differ from a plain program's by a relative error of at most 0.0041.
Values may be sent and summed in bfloat16 or wider, within the bound.
A program may use at most 64 MiB of HBM per device.

v0:
```python
import jax
import jax.numpy as jnp
from jax import lax
from jax.sharding import Mesh
from jax.sharding import PartitionSpec as P

ITERS = 3
OPT = ("opt_0", "opt_1", "opt_2")


first_coef = 3.4445
second_coef = -4.775
third_coef = 2.0315
epsilon = 1e-06
step_rate = 0.5
decay_rate = 0.1


def sent_to_all(shard, axis):
    size = lax.axis_size(axis)
    return lax.all_to_all(
        jnp.broadcast_to(shard[None], (size, *shard.shape)), axis, 0, 0, tiled=True
    )


def of_everyone(shard, axis):
    return sent_to_all(shard, axis).sum(axis=0)


def in_blocks(shard, dim, size):
    dims = shard.shape
    tiles = shard.reshape(*dims[:dim], size, dims[dim] // size, *dims[dim + 1 :])
    return jnp.moveaxis(tiles, dim, 0)


def laid_out(tiles, dim):
    tiles = jnp.moveaxis(tiles, 0, dim)
    dims = tiles.shape
    return tiles.reshape(*dims[:dim], dims[dim] * dims[dim + 1], *dims[dim + 2 :])


def turned_blocks(tiles, axes, order):
    inside = tiles.shape[1:]
    filled = tiles.reshape(*(lax.axis_size(a) for a in axes), *inside)
    for k in order:
        filled = lax.all_to_all(filled, axes[k], k, k, tiled=True)
    return filled.reshape(-1, *inside)


def two_step_exchange(shard, groups, order, split_dim, concat_dim):
    size = lax.axis_size(groups[0]) * lax.axis_size(groups[1])
    tiles = in_blocks(shard, split_dim, size)
    return laid_out(turned_blocks(tiles, groups, order), concat_dim)


def batched(first_matrix, second_matrix):
    return jnp.einsum("erk,ekc->erc", first_matrix, second_matrix, precision=lax.Precision.HIGHEST)


def identity_rows(row_count, gram_order):
    column_ids = lax.broadcasted_iota(jnp.int32, (row_count, gram_order), 1)
    row_ids = lax.broadcasted_iota(jnp.int32, (row_count, gram_order), 0)
    return (column_ids == row_ids).astype(jnp.float32)[None]


def newton_whole(gram_sum, trace_sum):
    identity_matrix = identity_rows(gram_sum.shape[1], gram_sum.shape[2])
    current = gram_sum / (trace_sum + epsilon)[:, None, None]
    accum = jnp.broadcast_to(identity_matrix, current.shape)
    for iteration in range(ITERS):
        squared = batched(current, current)
        polynomial = first_coef * identity_matrix + second_coef * current + third_coef * squared
        accum = batched(accum, polynomial)
        if iteration + 1 < ITERS:
            current = batched(batched(current, polynomial), polynomial)
    return accum


def on_device(momentum, weights):
    regrouped = lax.all_to_all(momentum, OPT, split_axis=1, concat_axis=2, tiled=True)[0]
    layers = lax.axis_size("layer")
    matrix_rows = regrouped.shape[1]
    gram_local = lax.dot_general(
        regrouped, regrouped, (((1,), (1,)), ((0,), (0,))), preferred_element_type=jnp.float32
    )
    gram_sum = of_everyone(gram_local, "layer")
    trace_sum = jnp.trace(gram_sum, axis1=1, axis2=2)
    accum = newton_whole(gram_sum, trace_sum)
    factor = (accum * jnp.sqrt(layers * matrix_rows / (trace_sum + epsilon))[:, None, None]).astype(
        jnp.bfloat16
    )
    update = lax.dot_general(
        regrouped, factor, (((2,), (1,)), ((0,), (0,))), preferred_element_type=jnp.float32
    )
    update = update.astype(jnp.bfloat16)[None]
    returned = two_step_exchange(update, (("opt_0", "opt_1"), "opt_2"), (1, 0), 2, 1)
    shrink = 1.0 - step_rate * decay_rate
    return (shrink * weights.astype(jnp.float32) - step_rate * returned.astype(jnp.float32)).astype(
        jnp.bfloat16
    )


def solution(mesh):
    split = Mesh(
        mesh.devices.reshape(8, 8, 2, mesh.shape["layer"]), ("opt_0", "opt_1", "opt_2", "layer")
    )
    in_specs = (P("layer", None, OPT, None), P("layer", None, OPT, None))
    out_specs = P("layer", None, OPT, None)
    return jax.shard_map(
        on_device, mesh=split, in_specs=in_specs, out_specs=out_specs, check_vma=False
    )
```

profile of v0, /device:TPU:1, one launch (start us, length us, event | category | flops | bytes accessed | tf_op | source)
XLA Modules:
  0.0 168.8 jit_solution(1840466125733119733)
XLA Ops:
  0.0 48.9 %all_to_all.24 = bf16[1,128,8,512]{3,2,0,1:T(8,128)(2,1)S(1)} all-to-all(bf16[1,128,8,512]{3,2,0,1:T(8,128)(2,1)} %bitcast.33), channel_id=1, replica_groups=mesh['opt_0'=8,'opt_1'=8,'opt_2'=2,'layer'=4] {'opt_0','opt_1','opt_2'}, dimensions={1} | all-to-all | bytes 2097152 | tf_op jit(solution)/shard_map/all_to_all | solution.py:80
  48.9 0.0 copy-start
  48.9 1.0 copy-done
  49.8 1.3 convolution_bitcast_fusion
  51.1 0.5 broadcast_in_dim.5
  51.7 50.4 %all_to_all.25 = f32[4,1,512,512]{3,2,1,0:T(8,128)} all-to-all(f32[4,1,512,512]{3,2,1,0:T(8,128)S(1)} %broadcast_in_dim.5), channel_id=1, replica_groups=mesh['opt_0'=8,'opt_1'=8,'opt_2'=2,'layer'=4] {'layer'}, dimensions={0} | all-to-all | bytes 8388608 | tf_op jit(solution)/shard_map/all_to_all | solution.py:21
  102.1 2.8 %reduce_sum.19 = f32[512,512]{1,0:T(8,128)S(1)} reduce(f32[4,1,512,512]{3,2,1,0:T(8,128)} %all_to_all.25, f32[]{:T(128)} %constant.5.clone.1), dimensions={0,1}, to_apply=%region_0.0 | reduce | flops 786432 | bytes 5242884 | tf_op jit(solution)/shard_map/reduce_sum | solution.py:27
  104.9 0.8 select_reduce_fusion
  106.4 1.9 %fusion.2 = f32[512,512]{1,0:T(8,128)S(1)} fusion(f32[512,512]{1,0:T(8,128)S(1)} %reduce_sum.19, f32[]{:T(128)S(6)} %add.29), kind=kOutput, calls=%fused_computation.12 | convolution fusion | flops 1612709888 | bytes 2097156 | tf_op jit(solution)/shard_map/erk,ekc->erc/dot_general | solution.py:57
  108.3 1.9 %fusion.10 = f32[512,512]{1,0:T(8,128)S(1)} fusion(f32[512,512]{1,0:T(8,128)S(1)} %fusion.2, f32[512,512]{1,0:T(8,128)S(1)} %reduce_sum.19, f32[]{:T(128)S(6)} %add.29), kind=kOutput, calls=%fused_computation.25 | convolution fusion | flops 1610874880 | bytes 3145732 | tf_op jit(solution)/shard_map/erk,ekc->erc/dot_general | solution.py:57
  110.2 1.1 fusion.9
  111.3 1.8 %fusion.11 = f32[512,512]{1,0:T(8,128)S(1)} fusion(f32[512,512]{1,0:T(8,128)S(1)} %fusion.10, f32[512,512]{1,0:T(8,128)S(1)} %fusion.2), kind=kOutput, calls=%fused_computation.26 | convolution fusion | flops 1610612736 | bytes 3145728 | tf_op jit(solution)/shard_map/erk,ekc->erc/dot_general | solution.py:57
  113.2 1.9 %fusion.1 = f32[512,512]{1,0:T(8,128)S(1)} fusion(f32[512,512]{1,0:T(8,128)S(1)} %fusion.11), kind=kOutput, calls=%fused_computation.10 | convolution fusion | flops 1612185600 | bytes 2097152 | tf_op jit(solution)/shard_map/erk,ekc->erc/dot_general | solution.py:57
  115.1 1.8 %fusion.13 = f32[512,512]{1,0:T(8,128)S(1)} fusion(f32[512,512]{1,0:T(8,128)S(1)} %fusion.11, f32[512,512]{1,0:T(8,128)S(1)} %fusion.1), kind=kOutput, calls=%fused_computation.28 | convolution fusion | flops 1610612736 | bytes 3145728 | tf_op jit(solution)/shard_map/erk,ekc->erc/dot_general | solution.py:57
  117.0 1.8 %fusion.14 = f32[512,512]{1,0:T(8,128)S(1)} fusion(f32[512,512]{1,0:T(8,128)S(1)} %fusion.13, f32[512,512]{1,0:T(8,128)S(1)} %fusion.1), kind=kOutput, calls=%fused_computation.29 | convolution fusion | flops 1610612736 | bytes 3145728 | tf_op jit(solution)/shard_map/erk,ekc->erc/dot_general | solution.py:57
  118.8 2.1 %fusion.12 = f32[512,512]{1,0:T(8,128)S(1)} fusion(f32[512,512]{1,0:T(8,128)S(1)} %fusion.9, f32[512,512]{1,0:T(8,128)S(1)} %fusion.1), kind=kOutput, calls=%fused_computation.27 | convolution fusion | flops 1610612736 | bytes 3145728 | tf_op jit(solution)/shard_map/erk,ekc->erc/dot_general | solution.py:57
  120.9 1.9 %fusion = f32[512,512]{1,0:T(8,128)S(1)} fusion(f32[512,512]{1,0:T(8,128)S(1)} %fusion.14), kind=kOutput, calls=%fused_computation.8 | convolution fusion | flops 1612185600 | bytes 2097152 | tf_op jit(solution)/shard_map/erk,ekc->erc/dot_general | solution.py:57
  122.8 0.0 copy-start.1
  122.8 1.9 %fusion.4 = bf16[512,512]{1,0:T(8,128)(2,1)S(1)} fusion(f32[512,512]{1,0:T(8,128)S(1)} %fusion.12, f32[512,512]{1,0:T(8,128)S(1)} %fusion, f32[]{:T(128)S(6)} %sqrt.4), kind=kOutput, calls=%fused_computation.15 | convolution fusion | flops 1611137024 | bytes 2621444 | tf_op jit(solution)/shard_map/erk,ekc->erc/dot_general | solution.py:57
  124.7 0.0 copy-done.1
  124.7 0.8 fusion.3
  125.4 0.5 copy.19
  126.0 0.1 copy.20
  126.1 7.4 %all_to_all.26 = bf16[64,2,1,1,8,512]{5,4,0,3,2,1:T(8,128)(2,1)S(1)} all-to-all(bf16[64,2,1,1,8,512]{5,4,0,3,2,1:T(8,128)(2,1)S(1)} %copy.20), channel_id=1, replica_groups=mesh['opt_0'=8,'opt_1'=8,'opt_2'=2,'layer'=4] {'opt_2'}, dimensions={1} | all-to-all | bytes 2097152 | tf_op jit(solution)/shard_map/all_to_all | solution.py:46
  133.5 0.1 copy.21
  133.7 32.5 %all_to_all.27 = bf16[64,2,1,1,8,512]{5,4,1,3,2,0:T(8,128)(2,1)S(1)} all-to-all(bf16[64,2,1,1,8,512]{5,4,1,3,2,0:T(8,128)(2,1)S(1)} %copy.21), channel_id=1, replica_groups=mesh['opt_0'=8,'opt_1'=8,'opt_2'=2,'layer'=4] {'opt_0','opt_1'}, dimensions={0} | all-to-all | bytes 2097152 | tf_op jit(solution)/shard_map/all_to_all | solution.py:46
  166.2 0.0 copy-start.2
  166.2 0.3 convert_multiply_fusion
  166.5 0.9 copy-done.2
  167.4 1.4 subtract_convert_fusion
Async XLA Ops:
  48.9 1.0 copy-start
  122.8 1.9 %copy-start.1 = (bf16[1,128,8,512]{3,2,0,1:T(8,128)(2,1)S(1)}, bf16[1,128,8,512]{3,2,0,1:T(8,128)(2,1)}, u32[]{:S(2)}) copy-start(bf16[1,128,8,512]{3,2,0,1:T(8,128)(2,1)} %copy-done) | copy-start | bytes 3145732
  166.2 1.2 copy-start.2
where the time goes:
time: 172 us; the launch traced here: 169 us
  blocking collectives  139 us (81%)
  matrix products  20.2 us (12%)
  other arithmetic  5.21 us (3%)
  local copies, waits for them, and re-layouts  3.2 us (2%)
    all_to_all x1, blocking collectives, sent_to_all(): lax.all_to_all(jnp.broadcast_to(shard[None], (size, *shard.shape)), axis,...  50.4 us
    all_to_all x1, blocking collectives, on_device(): lax.all_to_all(momentum, OPT, split_axis=1, concat_axis=2, tiled=True)[0]  48.9 us
    all_to_all x2, blocking collectives, turned_blocks(): filled = lax.all_to_all(filled, axes[k], k, k, tiled=True)  40 us
    dot_general x10, matrix products, batched(): jnp.einsum('erk,ekc->erc', first_matrix, second_matrix, precision=lax.Pre...  18.1 us

commit v1 on v0

--- a/solution.py
+++ b/solution.py
@@ -24,7 +24,11 @@
 
 
 def of_everyone(shard, axis):
-    return sent_to_all(shard, axis).sum(axis=0)
+    size = lax.axis_size(axis)
+    dims = shard.shape
+    slabs = shard.reshape(size, dims[-2] // size, dims[-1])
+    mine = lax.all_to_all(slabs, axis, 0, 0, tiled=True).sum(axis=0)
+    return sent_to_all(mine, axis).reshape(dims)
 
 
 def in_blocks(shard, dim, size):
@@ -54,7 +58,7 @@
 
 
 def batched(first_matrix, second_matrix):
-    return jnp.einsum("erk,ekc->erc", first_matrix, second_matrix, precision=lax.Precision.HIGHEST)
+    return jnp.einsum("erk,ekc->erc", first_matrix, second_matrix, precision=lax.Precision.HIGH)
 
 
 def identity_rows(row_count, gram_order):

time: 172 us -> 144 us (0.84)
  the two profiles are of different devices: /device:TPU:1 before, /device:TPU:16 now
where the time goes in v1:
time: 144 us; the launch traced here: 143 us
  blocking collectives  126 us (88%)
  matrix products  11.4 us (8%)
  other arithmetic  2.81 us (2%)
  local copies, waits for them, and re-layouts  2.53 us (2%)
    all_to_all x1, blocking collectives, on_device(): lax.all_to_all(momentum, OPT, split_axis=1, concat_axis=2, tiled=True)[0]  46.9 us
    all_to_all x2, blocking collectives, turned_blocks(): filled = lax.all_to_all(filled, axes[k], k, k, tiled=True)  44 us
    all_to_all x1, blocking collectives, of_everyone(): mine = lax.all_to_all(slabs, axis, 0, 0, tiled=True).sum(axis=0)  18.7 us
    all_to_all x1, blocking collectives, sent_to_all(): lax.all_to_all(jnp.broadcast_to(shard[None], (size, *shard.shape)), axis,...  15.9 us
    dot_general x10, matrix products, batched(): jnp.einsum('erk,ekc->erc', first_matrix, second_matrix, precision=lax.Pre...  9.92 us

profile of v1, /device:TPU:16, one launch (start us, length us, event | category | flops | bytes accessed | tf_op | source)
XLA Modules:
  0.0 143.2 jit_solution(436824465572541269)
XLA Ops:
  0.0 46.9 %all_to_all.29 = bf16[1,128,8,512]{3,2,0,1:T(8,128)(2,1)S(1)} all-to-all(bf16[1,128,8,512]{3,2,0,1:T(8,128)(2,1)} %bitcast.44), channel_id=1, replica_groups=mesh['opt_0'=8,'opt_1'=8,'opt_2'=2,'layer'=4] {'opt_0','opt_1','opt_2'}, dimensions={1} | all-to-all | bytes 2097152 | tf_op jit(solution)/shard_map/all_to_all | solution.py:84
  46.9 0.0 copy-start
  46.9 0.5 copy.12
  47.4 0.7 fusion.5
  48.1 0.0 copy-done
  48.2 18.7 %all_to_all.30 = f32[4,128,512]{2,1,0:T(8,128)S(1)} all-to-all(f32[4,128,512]{2,1,0:T(8,128)S(1)} %fusion.5), channel_id=1, replica_groups=mesh['opt_0'=8,'opt_1'=8,'opt_2'=2,'layer'=4] {'layer'}, dimensions={0} | all-to-all | bytes 2097152 | tf_op jit(solution)/shard_map/all_to_all | solution.py:30
  66.9 0.1 reduce_sum.19
  67.0 0.1 broadcast_in_dim.9
  67.1 15.9 %all_to_all.31 = f32[4,128,512]{2,1,0:T(8,128)S(1)} all-to-all(f32[4,128,512]{2,1,0:T(8,128)S(1)} %broadcast_in_dim.9), channel_id=1, replica_groups=mesh['opt_0'=8,'opt_1'=8,'opt_2'=2,'layer'=4] {'layer'}, dimensions={0} | all-to-all | bytes 2097152 | tf_op jit(solution)/shard_map/all_to_all | solution.py:21
  83.0 0.7 select_reduce_fusion
  84.4 0.3 broadcast_multiply_fusion
  84.7 1.0 fusion.2
  85.7 1.0 fusion.9
  86.8 0.7 fusion.8
  87.6 1.0 fusion.10
  88.6 1.1 fusion.1
  89.7 1.0 fusion.12
  90.7 1.0 fusion.13
  91.7 1.0 fusion.11
  92.7 1.1 fusion
  93.8 0.0 copy-start.1
  93.8 1.0 fusion.4
  94.8 0.2 copy-done.1
  95.0 0.8 fusion.3
  95.8 0.5 copy.9
  96.3 0.1 copy.10
  96.4 4.6 %all_to_all.32 = bf16[64,2,1,1,8,512]{5,4,0,3,2,1:T(8,128)(2,1)S(1)} all-to-all(bf16[64,2,1,1,8,512]{5,4,0,3,2,1:T(8,128)(2,1)S(1)} %copy.10), channel_id=1, replica_groups=mesh['opt_0'=8,'opt_1'=8,'opt_2'=2,'layer'=4] {'opt_2'}, dimensions={1} | all-to-all | bytes 2097152 | tf_op jit(solution)/shard_map/all_to_all | solution.py:50
  101.0 0.1 copy.11
  101.1 39.4 %all_to_all.33 = bf16[64,2,1,1,8,512]{5,4,1,3,2,0:T(8,128)(2,1)S(1)} all-to-all(bf16[64,2,1,1,8,512]{5,4,1,3,2,0:T(8,128)(2,1)S(1)} %copy.11), channel_id=1, replica_groups=mesh['opt_0'=8,'opt_1'=8,'opt_2'=2,'layer'=4] {'opt_0','opt_1'}, dimensions={0} | all-to-all | bytes 2097152 | tf_op jit(solution)/shard_map/all_to_all | solution.py:50
  140.6 0.0 copy-start.2
  140.6 0.3 convert_multiply_fusion
  140.9 0.9 copy-done.2
  141.8 1.4 subtract_convert_fusion
Async XLA Ops:
  46.9 1.2 copy-start
  93.8 1.2 copy-start.1
  140.6 1.2 copy-start.2

commit v2 on v0

v2 whole, which is shorter than its diff:
```python
import functools

import jax
import jax.numpy as jnp
from jax import lax
from jax.experimental import pallas as pl
from jax.experimental.pallas import tpu as pltpu
from jax.sharding import PartitionSpec as P

ITERS = 3
MESH = pl.DeviceIdType.MESH
DMA = pltpu.SemaphoreType.DMA

first_coef = 3.4445
second_coef = -4.775
third_coef = 2.0315
epsilon = 1e-06
step_rate = 0.5
decay_rate = 0.1
shrink = 1.0 - step_rate * decay_rate

B = 128


def signed(k):
    half = (k + 1) // 2
    return jnp.where(lax.rem(k, 2) == 1, half, lax.rem(8 - half, 8))


def target(y, z, k):
    return lax.rem(y + signed(k // 8), 8) * 8 + lax.rem(z + signed(lax.rem(k, 8)), 8)


def dot(a, b):
    return jnp.dot(a, b, preferred_element_type=jnp.float32)


def split(value, ref, cols):
    high = value.astype(jnp.bfloat16)
    ref[0, :, cols] = high
    ref[1, :, cols] = (value - high.astype(jnp.float32)).astype(jnp.bfloat16)


def product(a_ref, b_ref, finish, width=256):
    n = a_ref.shape[1]
    left = jnp.concatenate([a_ref[0], a_ref[1], a_ref[0]], axis=1)
    for j in range(n // width):
        cols = pl.ds(j * width, width)
        right = jnp.concatenate([b_ref[0, :, cols], b_ref[0, :, cols], b_ref[1, :, cols]], axis=0)
        finish(dot(left, right), cols, j * width)


def unit(rows, width, start):
    r = lax.broadcasted_iota(jnp.int32, (rows, width), 0)
    c = lax.broadcasted_iota(jnp.int32, (rows, width), 1)
    return (r == c + start).astype(jnp.float32)


def step_kernel(m_ref, w_ref, o_ref, inb, upd, ub, wv, mat, g, ra, g2, rb, cur, cs, ps, qs, acs, fac,
                in_send, in_recv, w_sem, x_send, x_recv, out_send, out_recv):
    opt, x = lax.axis_index("opt"), lax.axis_index("layer")
    layers = 4
    chip, c = opt // 2, lax.rem(opt, 2)
    y, z = chip // 8, lax.rem(chip, 8)
    near = (x + 1 - 2 * lax.rem(x, 2), layers - 1 - x)

    pltpu.make_async_copy(m_ref.at[chip, c], inb.at[chip, c], in_recv).start()
    pltpu.make_async_copy(w_ref, wv, w_sem).start()

    barrier = pltpu.get_barrier_semaphore()

    def greet(k, carry):
        pl.semaphore_signal(barrier, inc=1, device_id=(lax.rem(opt + k, 128), x), device_id_type=MESH)
        return carry

    lax.fori_loop(1, 128, greet, 0)
    for other in near:
        pl.semaphore_signal(barrier, inc=1, device_id=(opt, other), device_id_type=MESH)
    pl.semaphore_wait(barrier, 129)

    for core in range(2):
        def give(k, carry):
            t = target(y, z, k)

            @pl.when((t * 2 + core) != opt)
            def _():
                pltpu.make_async_remote_copy(
                    m_ref.at[t, core], inb.at[chip, c], in_send, in_recv,
                    device_id=(t * 2 + core, x), device_id_type=MESH,
                ).start()
            return carry

        lax.fori_loop(0, 64, give, 0)
    pltpu.make_async_copy(inb, inb, in_recv).wait()

    def lay(i, carry):
        rows = inb[pl.ds(i * 4, 4)].astype(jnp.float32).reshape(64, 512)
        mat[pl.ds(pl.multiple_of(i * 64, 64), 64), :] = rows.astype(jnp.bfloat16)
        return carry

    lax.fori_loop(0, 16, lay, 0)

    def gram(lo, hi, start):
        return lax.dot_general(mat[:, lo:hi], mat[:, start:], (((0,), (0,)), ((), ())), preferred_element_type=jnp.float32)

    top = gram(0, 256, 0)
    g[0, :, 0:512] = top[0:128]
    g[1, :, 0:384] = top[128:256, 128:]
    low = gram(256, 512, 256)
    g[1, :, 384:640] = low[0:128]
    g[0, :, 512:640] = low[128:256, 128:]

    def exchange(src, dst, stage, half):
        other = near[(stage + half) % 2]
        return pltpu.make_async_remote_copy(
            src.at[half], dst.at[half], x_send.at[stage, half], x_recv.at[stage, half],
            device_id=(opt, other), device_id_type=MESH,
        )

    for half in range(2):
        exchange(g, ra, 0, half).start()
    for half in range(2):
        exchange(g, ra, 0, half).wait_recv()
        g2[half] = g[half] + ra[half]
        exchange(g2, rb, 1, half).start()
    for half in range(2):
        exchange(g2, rb, 1, half).wait_recv()

    where = {0: (0, 0), 1: (1, 0), 2: (1, 384), 3: (0, 512)}

    def block(i, j):
        half, base = where[i]
        cols = slice(base + (j - i) * B, base + (j - i + 1) * B)
        return g2[half, :, cols] + rb[half, :, cols]

    eye = unit(B, B, 0)
    diagonal = jnp.zeros((B, B), jnp.float32)
    for i in range(4):
        for j in range(i, 4):
            blk = block(i, j)
            cur[i * B:(i + 1) * B, j * B:(j + 1) * B] = blk
            if i == j:
                diagonal = diagonal + blk * eye
            else:
                cur[j * B:(j + 1) * B, i * B:(i + 1) * B] = blk.T
    trace = jnp.sum(jnp.sum(diagonal, axis=0, keepdims=True), axis=1, keepdims=True) + epsilon
    scale = 1.0 / trace
    for j in range(2):
        cols = pl.ds(j * 256, 256)
        value = cur[:, cols] * scale
        cur[:, cols] = value
        split(value, cs, cols)

    def poly(panel, cols, start):
        value = first_coef * unit(512, 256, start) + second_coef * cur[:, cols] + third_coef * panel
        split(value, ps, cols)
        return value

    def keep_current(panel, cols, start):
        cur[:, cols] = panel
        split(panel, cs, cols)

    product(cs, cs, poly)
    product(cs, ps, lambda v, cols, start: split(v, qs, cols))
    product(qs, ps, keep_current)
    for h in range(2):
        acs[h] = ps[h]
    product(cs, cs, poly)
    product(acs, ps, lambda v, cols, start: split(v, acs2(acs), cols))
    product(cs, ps, lambda v, cols, start: split(v, qs, cols))
    product(qs, ps, keep_current)
    product(cs, cs, poly)
    root = jnp.sqrt((layers * 1024) / trace)

    def last(v, cols, start):
        fac[:, cols] = (v * root).astype(jnp.bfloat16)

    product(acs2(acs), ps, last)

    def update(i, carry):
        rows = mat[pl.ds(pl.multiple_of(i * 256, 256), 256), :]
        upd[pl.ds(i * 16, 16)] = dot(rows, fac[...]).reshape(16, 2, 8, 512).astype(jnp.bfloat16)
        return carry

    lax.fori_loop(0, 4, update, 0)

    pltpu.make_async_copy(upd.at[chip, c], ub.at[chip, c], out_recv.at[c]).start()

    def give_back(k, carry):
        t = target(y, z, k)
        for core in range(2):
            @pl.when((t * 2 + core) != opt)
            def _(core=core):
                pltpu.make_async_remote_copy(
                    upd.at[t, core], ub.at[chip, c], out_send, out_recv.at[c],
                    device_id=(t * 2 + core, x), device_id_type=MESH,
                ).start()
        return carry

    lax.fori_loop(0, 64, give_back, 0)

    pltpu.make_async_copy(w_ref, wv, w_sem).wait()
    for core in range(2):
        pltpu.make_async_copy(ub.at[:, core], ub.at[:, core], out_recv.at[core]).wait()

        def finish(i, carry):
            rows = pl.ds(i * 8, 8)
            old = wv[rows, core].astype(jnp.float32)
            o_ref[rows, core] = (shrink * old - step_rate * ub[rows, core].astype(jnp.float32)).astype(jnp.bfloat16)
            return carry

        lax.fori_loop(0, 8, finish, 0)

    sent = pl.ds(0, 63)
    for sem, buf in ((in_send, inb), (out_send, ub)):
        pltpu.make_async_copy(buf.at[sent], buf.at[sent], sem).wait()
        pltpu.make_async_copy(buf.at[0, 0], buf.at[0, 0], sem).wait()
    for half in range(2):
        exchange(g, ra, 0, half).wait_send()
        exchange(g2, rb, 1, half).wait_send()


class acs2:
    def __init__(self, ref):
        self.ref = ref
        self.shape = ref.shape

    def __getitem__(self, at):
        at = at if isinstance(at, tuple) else (at,)
        return self.ref[(at[0] + 2, *at[1:])]

    def __setitem__(self, at, value):
        self.ref[(at[0] + 2, *at[1:])] = value


def on_device(momentum, weights):
    places = (64, 2, 8, 512)
    bf, f4 = jnp.bfloat16, jnp.float32
    out = pl.pallas_call(
        step_kernel,
        name="orthogonal_step",
        out_shape=jax.ShapeDtypeStruct(places, bf),
        in_specs=[pl.BlockSpec(memory_space=pl.ANY)] * 2,
        out_specs=pl.BlockSpec(memory_space=pltpu.VMEM),
        scratch_shapes=[
            *[pltpu.VMEM(places, bf)] * 4,
            pltpu.VMEM((1024, 512), bf),
            *[pltpu.VMEM((2, B, 640), f4)] * 4,
            pltpu.VMEM((512, 512), f4),
            *[pltpu.VMEM((2, 512, 512), bf)] * 3,
            pltpu.VMEM((4, 512, 512), bf),
            pltpu.VMEM((512, 512), bf),
            DMA, DMA, DMA, DMA((2, 2)), DMA((2, 2)), DMA, DMA((2,)),
        ],
        compiler_params=pltpu.CompilerParams(collective_id=0, has_side_effects=True, vmem_limit_bytes=56 * 2**20),
    )(momentum.reshape(places), weights.reshape(places))
    return out.reshape(momentum.shape)


def solution(mesh):
    spec = P("layer", None, "opt", None)
    return jax.shard_map(on_device, mesh=mesh, in_specs=(spec, spec), out_specs=spec, check_vma=False)
```

time: 172 us -> 97.6 us (0.57); the launches traced: 169 us -> 96.2 us
  blocking collectives: 139 us -> 0 us
  Pallas kernels: 0 us -> 93.9 us
  matrix products: 20.2 us -> 0 us
  other arithmetic: 5.21 us -> 0 us
    all_to_all x4 -> x0, blocking collectives: 139 us -> none  [the longest x1 50.4 us: sent_to_all(): lax.all_to_all(jnp.broadcast_to(shard[None], (size, *shard.shape)), axis,...]
    pallas_call x0 -> x1, Pallas kernels: none -> 93.9 us  [on_device(): pl.pallas_call(step_kernel, name='orthogonal_step', out_shape=jax.ShapeDt...]
    dot_general x12 -> x0, matrix products: 20.2 us -> none  [the longest x10 18.1 us: batched(): jnp.einsum('erk,ekc->erc', first_matrix, second_matrix, precision=lax.Pre...]
    reduce_sum x2 -> x0, other arithmetic: 3.53 us -> none  [the longest x1 2.78 us: of_everyone(): return sent_to_all(shard, axis).sum(axis=0)]
where the time goes in v2:
time: 97.6 us; the launch traced here: 96.2 us
  Pallas kernels  93.9 us (96%)
  local copies, waits for them, and re-layouts  2.26 us (2%)
    pallas_call x1, Pallas kernels, on_device(): pl.pallas_call(step_kernel, name='orthogonal_step', out_shape=jax.ShapeDt...  93.9 us
    unnamed x1, local copies, waits for them, and re-layouts  2.26 us

profile of v2, /device:TPU:1, one launch (start us, length us, event | category | flops | bytes accessed | tf_op | source)
XLA Modules:
  0.0 96.2 jit_solution(8909495673375074811)
XLA Ops:
  0.0 93.9 %orthogonal_step.1 = bf16[64,2,8,512]{3,2,1,0:T(8,128)(2,1)} custom-call(bf16[64,2,8,512]{3,2,1,0:T(8,128)(2,1)} %bitcast.4, bf16[64,2,8,512]{3,2,1,0:T(8,128)(2,1)} %bitcast.5), custom_call_target="tpu_custom_call" | custom-call | tf_op jit(solution)/shard_map/orthogonal_step/pallas_call | solution.py:239
  93.9 2.3 %copy.4 = bf16[1,128,8,512]{3,2,1,0:T(8,128)(2,1)} copy(bf16[1,128,8,512]{3,2,1,0:T(8,128)(2,1)} %bitcast.3) | data formatting | bytes 2097152

commit v3 on v2

--- a/solution.py
+++ b/solution.py
@@ -20,6 +20,8 @@
 shrink = 1.0 - step_rate * decay_rate
 
 B = 128
+WINDOW = 3
+HELD = 6
 
 
 def signed(k):
@@ -27,8 +29,12 @@
     return jnp.where(lax.rem(k, 2) == 1, half, lax.rem(8 - half, 8))
 
 
-def target(y, z, k):
-    return lax.rem(y + signed(k // 8), 8) * 8 + lax.rem(z + signed(lax.rem(k, 8)), 8)
+def target(y, z, odd, k):
+    row, j = k // 4, lax.rem(k, 4)
+    dy = signed(row)
+    turn = lax.rem(y + z + dy + odd, 2)
+    dz = signed(jnp.where(turn == 1, j + j // 2 * 2 + 1, j + (j + 1) // 2 * 2))
+    return lax.rem(y + dy, 8) * 8 + lax.rem(z + dz, 8)
 
 
 def dot(a, b):
@@ -56,16 +62,16 @@
     return (r == c + start).astype(jnp.float32)
 
 
-def step_kernel(m_ref, w_ref, o_ref, inb, upd, ub, wv, mat, g, ra, g2, rb, cur, cs, ps, qs, acs, fac,
-                in_send, in_recv, w_sem, x_send, x_recv, out_send, out_recv):
+def step_kernel(m_ref, ub, inb, upd, spare, mat, g, ra, g2, rb, cur, cs, ps, qs, acs, fac,
+                own, in_send, in_recv, x_send, x_recv, out_send, out_recv):
     opt, x = lax.axis_index("opt"), lax.axis_index("layer")
     layers = 4
     chip, c = opt // 2, lax.rem(opt, 2)
     y, z = chip // 8, lax.rem(chip, 8)
     near = (x + 1 - 2 * lax.rem(x, 2), layers - 1 - x)
 
-    pltpu.make_async_copy(m_ref.at[chip, c], inb.at[chip, c], in_recv).start()
-    pltpu.make_async_copy(w_ref, wv, w_sem).start()
+    pltpu.make_async_copy(m_ref.at[opt], inb.at[opt], own).start()
+    pltpu.make_async_copy(m_ref.at[opt], spare, in_send.at[2 * (2 * c + lax.rem(y + z, 2))]).start()
 
     barrier = pltpu.get_barrier_semaphore()
 
@@ -78,23 +84,46 @@
         pl.semaphore_signal(barrier, inc=1, device_id=(opt, other), device_id_type=MESH)
     pl.semaphore_wait(barrier, 129)
 
-    for core in range(2):
-        def give(k, carry):
-            t = target(y, z, k)
-
-            @pl.when((t * 2 + core) != opt)
+    def give(group):
+        def one(k, carry):
+            d = target(y, z, lax.rem(group // 2, 2), k) * 2 + group // 4
+
+            @pl.when(d != opt)
             def _():
                 pltpu.make_async_remote_copy(
-                    m_ref.at[t, core], inb.at[chip, c], in_send, in_recv,
-                    device_id=(t * 2 + core, x), device_id_type=MESH,
+                    m_ref.at[d], inb.at[opt], in_send.at[group], in_recv,
+                    device_id=(d, x), device_id_type=MESH,
                 ).start()
             return carry
 
-        lax.fori_loop(0, 64, give, 0)
-    pltpu.make_async_copy(inb, inb, in_recv).wait()
+        start = lax.rem(group, 2) * 16
+        lax.fori_loop(start, start + 16, one, 0)
+
+    def given(group):
+        sent = inb.at[pl.ds(0, 16)]
+        pltpu.make_async_copy(sent, sent, in_send.at[group]).wait()
+
+    def give_next(group, carry):
+        given(group - WINDOW)
+        give(group)
+        return carry
+
+    def first(group, carry):
+        give(group)
+        return carry
+
+    lax.fori_loop(0, WINDOW, first, 0)
+    lax.fori_loop(WINDOW, HELD, give_next, 0)
+
+    @pl.when(c == 1)
+    def _():
+        lax.fori_loop(HELD, 8, give_next, 0)
+
+    pltpu.make_async_copy(inb.at[pl.ds(0, 127)], inb.at[pl.ds(0, 127)], in_recv).wait()
+    pltpu.make_async_copy(inb.at[0], inb.at[0], own).wait()
 
     def lay(i, carry):
-        rows = inb[pl.ds(i * 4, 4)].astype(jnp.float32).reshape(64, 512)
+        rows = inb[pl.ds(i * 8, 8)].astype(jnp.float32).reshape(64, 512)
         mat[pl.ds(pl.multiple_of(i * 64, 64), 64), :] = rows.astype(jnp.bfloat16)
         return carry
 
@@ -119,6 +148,11 @@
 
     for half in range(2):
         exchange(g, ra, 0, half).start()
+
+    @pl.when(c == 0)
+    def _():
+        lax.fori_loop(HELD, 8, give_next, 0)
+
     for half in range(2):
         exchange(g, ra, 0, half).wait_recv()
         g2[half] = g[half] + ra[half]
@@ -179,45 +213,38 @@
 
     def update(i, carry):
         rows = mat[pl.ds(pl.multiple_of(i * 256, 256), 256), :]
-        upd[pl.ds(i * 16, 16)] = dot(rows, fac[...]).reshape(16, 2, 8, 512).astype(jnp.bfloat16)
+        upd[pl.ds(i * 32, 32)] = dot(rows, fac[...]).reshape(32, 8, 512).astype(jnp.bfloat16)
         return carry
 
     lax.fori_loop(0, 4, update, 0)
 
-    pltpu.make_async_copy(upd.at[chip, c], ub.at[chip, c], out_recv.at[c]).start()
+    pltpu.make_async_copy(upd.at[opt], ub.at[opt], own).start()
 
     def give_back(k, carry):
-        t = target(y, z, k)
-        for core in range(2):
-            @pl.when((t * 2 + core) != opt)
-            def _(core=core):
-                pltpu.make_async_remote_copy(
-                    upd.at[t, core], ub.at[chip, c], out_send, out_recv.at[c],
-                    device_id=(t * 2 + core, x), device_id_type=MESH,
-                ).start()
-        return carry
-
-    lax.fori_loop(0, 64, give_back, 0)
-
-    pltpu.make_async_copy(w_ref, wv, w_sem).wait()
-    for core in range(2):
-        pltpu.make_async_copy(ub.at[:, core], ub.at[:, core], out_recv.at[core]).wait()
-
-        def finish(i, carry):
-            rows = pl.ds(i * 8, 8)
-            old = wv[rows, core].astype(jnp.float32)
-            o_ref[rows, core] = (shrink * old - step_rate * ub[rows, core].astype(jnp.float32)).astype(jnp.bfloat16)
-            return carry
-
-        lax.fori_loop(0, 8, finish, 0)
-
-    sent = pl.ds(0, 63)
-    for sem, buf in ((in_send, inb), (out_send, ub)):
-        pltpu.make_async_copy(buf.at[sent], buf.at[sent], sem).wait()
-        pltpu.make_async_copy(buf.at[0, 0], buf.at[0, 0], sem).wait()
+        d = target(y, z, lax.rem(k // 2, 2), k // 4) * 2 + lax.rem(k, 2)
+
+        @pl.when(d != opt)
+        def _():
+            pltpu.make_async_remote_copy(
+                upd.at[d], ub.at[opt], out_send, out_recv,
+                device_id=(d, x), device_id_type=MESH,
+            ).start()
+        return carry
+
+    lax.fori_loop(0, 128, give_back, 0)
+
+    def sent(group, carry):
+        given(group)
+        return carry
+
+    lax.fori_loop(8 - WINDOW, 8, sent, 0)
     for half in range(2):
         exchange(g, ra, 0, half).wait_send()
         exchange(g2, rb, 1, half).wait_send()
+    others = pl.ds(0, 127)
+    pltpu.make_async_copy(upd.at[others], upd.at[others], out_send).wait()
+    pltpu.make_async_copy(ub.at[others], ub.at[others], out_recv).wait()
+    pltpu.make_async_copy(upd.at[0], upd.at[0], own).wait()
 
 
 class acs2:
@@ -234,27 +261,29 @@
 
 
 def on_device(momentum, weights):
-    places = (64, 2, 8, 512)
+    places = (128, 8, 512)
     bf, f4 = jnp.bfloat16, jnp.float32
-    out = pl.pallas_call(
+    update = pl.pallas_call(
         step_kernel,
-        name="orthogonal_step",
+        name="orthogonal_update",
         out_shape=jax.ShapeDtypeStruct(places, bf),
-        in_specs=[pl.BlockSpec(memory_space=pl.ANY)] * 2,
-        out_specs=pl.BlockSpec(memory_space=pltpu.VMEM),
+        in_specs=[pl.BlockSpec(memory_space=pl.ANY)],
+        out_specs=pl.BlockSpec(memory_space=pl.ANY),
         scratch_shapes=[
-            *[pltpu.VMEM(places, bf)] * 4,
+            *[pltpu.VMEM(places, bf)] * 2,
+            pltpu.VMEM((8, 512), bf),
             pltpu.VMEM((1024, 512), bf),
             *[pltpu.VMEM((2, B, 640), f4)] * 4,
             pltpu.VMEM((512, 512), f4),
             *[pltpu.VMEM((2, 512, 512), bf)] * 3,
             pltpu.VMEM((4, 512, 512), bf),
             pltpu.VMEM((512, 512), bf),
-            DMA, DMA, DMA, DMA((2, 2)), DMA((2, 2)), DMA, DMA((2,)),
+            DMA, DMA((8,)), DMA, DMA((2, 2)), DMA((2, 2)), DMA, DMA,
         ],
         compiler_params=pltpu.CompilerParams(collective_id=0, has_side_effects=True, vmem_limit_bytes=56 * 2**20),
-    )(momentum.reshape(places), weights.reshape(places))
-    return out.reshape(momentum.shape)
+    )(momentum.reshape(places))
+    update = update.reshape(weights.shape).astype(jnp.float32)
+    return (shrink * weights.astype(jnp.float32) - step_rate * update).astype(jnp.bfloat16)
 
 
 def solution(mesh):

time: 97.6 us -> 104 us (1.066)
  Pallas kernels: 93.9 us -> 101 us
  other arithmetic: 0 us -> 2.58 us
  local copies, waits for them, and re-layouts: 2.26 us -> 0.01 us
    pallas_call x1, Pallas kernels: 93.9 us -> 101 us  [on_device(): pl.pallas_call(step_kernel, name='orthogonal_update', out_shape=jax.Shape...]
    convert_element_type x0 -> x1, other arithmetic: none -> 2.58 us  [on_device(): (shrink * weights.astype(jnp.float32) - step_rate * update).astype(jnp.bf...]
    unnamed x1 -> x2, local copies, waits for them, and re-layouts: 2.26 us -> 0.01 us
where the time goes in v3:
time: 104 us; the launch traced here: 103 us
  Pallas kernels  101 us (97%)
  other arithmetic  2.58 us (2%)
    pallas_call x1, Pallas kernels, on_device(): pl.pallas_call(step_kernel, name='orthogonal_update', out_shape=jax.Shape...  101 us
    convert_element_type x1, other arithmetic, on_device(): (shrink * weights.astype(jnp.float32) - step_rate * update).astype(jnp.bf...  2.58 us

profile of v3, /device:TPU:1, one launch (start us, length us, event | category | flops | bytes accessed | tf_op | source)
XLA Modules:
  0.0 103.3 jit_solution(17739112306405294697)
XLA Ops:
  0.0 0.0 copy-start
  0.0 100.7 %orthogonal_update.1 = bf16[128,8,512]{2,1,0:T(8,128)(2,1)} custom-call(bf16[128,8,512]{2,1,0:T(8,128)(2,1)} %bitcast.5), custom_call_target="tpu_custom_call" | custom-call | tf_op jit(solution)/shard_map/orthogonal_update/pallas_call | solution.py:266
  100.7 0.0 copy-done
  100.7 2.6 %fusion = bf16[1,128,8,512]{3,2,1,0:T(8,128)(2,1)} fusion(bf16[128,8,512]{2,1,0:T(8,128)(2,1)} %orthogonal_update.1, bf16[1,128,8,512]{3,2,1,0:T(8,128)(2,1)S(1)} %copy-done), kind=kLoop, calls=%fused_computation.1 | loop fusion | flops 3145728 | bytes 3145728 | tf_op jit(solution)/shard_map/convert_element_type | solution.py:286
Async XLA Ops:
  0.0 100.7 %copy-start = (bf16[1,128,8,512]{3,2,1,0:T(8,128)(2,1)S(1)}, bf16[1,128,8,512]{3,2,1,0:T(8,128)(2,1)}, u32[]{:S(2)}) copy-start(bf16[1,128,8,512]{3,2,1,0:T(8,128)(2,1)} %param.3) | copy-start | bytes 3145732

commit v4 on v3

--- a/solution.py
+++ b/solution.py
@@ -20,21 +20,19 @@
 shrink = 1.0 - step_rate * decay_rate
 
 B = 128
-WINDOW = 3
-HELD = 6
-
-
-def signed(k):
-    half = (k + 1) // 2
-    return jnp.where(lax.rem(k, 2) == 1, half, lax.rem(8 - half, 8))
-
-
-def target(y, z, odd, k):
-    row, j = k // 4, lax.rem(k, 4)
-    dy = signed(row)
-    turn = lax.rem(y + z + dy + odd, 2)
-    dz = signed(jnp.where(turn == 1, j + j // 2 * 2 + 1, j + (j + 1) // 2 * 2))
-    return lax.rem(y + dy, 8) * 8 + lax.rem(z + dz, 8)
+
+
+TURNS = (4, 5, 3, 6, 2, 7, 1, 0)
+
+
+def turn_of(k):
+    half = (8 - k) // 2
+    return jnp.where(lax.rem(k, 2) == 1, 8 - half, half)
+
+
+def ahead(at, turn):
+    there = at + turn
+    return jnp.where(there >= 8, there - 8, there)
 
 
 def dot(a, b):
@@ -62,7 +60,7 @@
     return (r == c + start).astype(jnp.float32)
 
 
-def step_kernel(m_ref, ub, inb, upd, spare, mat, g, ra, g2, rb, cur, cs, ps, qs, acs, fac,
+def step_kernel(m_ref, ub, inb, upd, mat, g, ra, g2, rb, cur, cs, ps, qs, acs, fac,
                 own, in_send, in_recv, x_send, x_recv, out_send, out_recv):
     opt, x = lax.axis_index("opt"), lax.axis_index("layer")
     layers = 4
@@ -71,7 +69,6 @@
     near = (x + 1 - 2 * lax.rem(x, 2), layers - 1 - x)
 
     pltpu.make_async_copy(m_ref.at[opt], inb.at[opt], own).start()
-    pltpu.make_async_copy(m_ref.at[opt], spare, in_send.at[2 * (2 * c + lax.rem(y + z, 2))]).start()
 
     barrier = pltpu.get_barrier_semaphore()
 
@@ -84,40 +81,26 @@
         pl.semaphore_signal(barrier, inc=1, device_id=(opt, other), device_id_type=MESH)
     pl.semaphore_wait(barrier, 129)
 
-    def give(group):
-        def one(k, carry):
-            d = target(y, z, lax.rem(group // 2, 2), k) * 2 + group // 4
-
-            @pl.when(d != opt)
-            def _():
-                pltpu.make_async_remote_copy(
-                    m_ref.at[d], inb.at[opt], in_send.at[group], in_recv,
-                    device_id=(d, x), device_id_type=MESH,
-                ).start()
-            return carry
-
-        start = lax.rem(group, 2) * 16
-        lax.fori_loop(start, start + 16, one, 0)
-
-    def given(group):
-        sent = inb.at[pl.ds(0, 16)]
-        pltpu.make_async_copy(sent, sent, in_send.at[group]).wait()
-
-    def give_next(group, carry):
-        given(group - WINDOW)
-        give(group)
-        return carry
-
-    def first(group, carry):
-        give(group)
-        return carry
-
-    lax.fori_loop(0, WINDOW, first, 0)
-    lax.fori_loop(WINDOW, HELD, give_next, 0)
-
-    @pl.when(c == 1)
-    def _():
-        lax.fori_loop(HELD, 8, give_next, 0)
+    columns = [ahead(z, turn) * 2 for turn in TURNS]
+
+    def send(src, dst, sent, landed, d, place):
+        def start():
+            pltpu.make_async_remote_copy(
+                src.at[d], dst.at[opt], sent, landed, device_id=(d, x), device_id_type=MESH
+            ).start()
+
+        if place == 7:
+            pl.when(d != opt)(start)
+        else:
+            start()
+
+    def give(k, carry):
+        row = ahead(y, turn_of(lax.rem(k, 8))) * 16 + k // 8
+        for place, column in enumerate(columns):
+            send(m_ref, inb, in_send, in_recv, row + column, place)
+        return carry
+
+    lax.fori_loop(0, 16, give, 0)
 
     pltpu.make_async_copy(inb.at[pl.ds(0, 127)], inb.at[pl.ds(0, 127)], in_recv).wait()
     pltpu.make_async_copy(inb.at[0], inb.at[0], own).wait()
@@ -148,10 +131,6 @@
 
     for half in range(2):
         exchange(g, ra, 0, half).start()
-
-    @pl.when(c == 0)
-    def _():
-        lax.fori_loop(HELD, 8, give_next, 0)
 
     for half in range(2):
         exchange(g, ra, 0, half).wait_recv()
@@ -221,27 +200,19 @@
     pltpu.make_async_copy(upd.at[opt], ub.at[opt], own).start()
 
     def give_back(k, carry):
-        d = target(y, z, lax.rem(k // 2, 2), k // 4) * 2 + lax.rem(k, 2)
-
-        @pl.when(d != opt)
-        def _():
-            pltpu.make_async_remote_copy(
-                upd.at[d], ub.at[opt], out_send, out_recv,
-                device_id=(d, x), device_id_type=MESH,
-            ).start()
-        return carry
-
-    lax.fori_loop(0, 128, give_back, 0)
-
-    def sent(group, carry):
-        given(group)
-        return carry
-
-    lax.fori_loop(8 - WINDOW, 8, sent, 0)
+        row = ahead(y, turn_of(k)) * 16
+        for place, column in enumerate(columns):
+            for core in range(2):
+                send(upd, ub, out_send, out_recv, row + column + core, place)
+        return carry
+
+    lax.fori_loop(0, 8, give_back, 0)
+
     for half in range(2):
         exchange(g, ra, 0, half).wait_send()
         exchange(g2, rb, 1, half).wait_send()
     others = pl.ds(0, 127)
+    pltpu.make_async_copy(inb.at[others], inb.at[others], in_send).wait()
     pltpu.make_async_copy(upd.at[others], upd.at[others], out_send).wait()
     pltpu.make_async_copy(ub.at[others], ub.at[others], out_recv).wait()
     pltpu.make_async_copy(upd.at[0], upd.at[0], own).wait()
@@ -267,20 +238,19 @@
         step_kernel,
         name="orthogonal_update",
         out_shape=jax.ShapeDtypeStruct(places, bf),
-        in_specs=[pl.BlockSpec(memory_space=pl.ANY)],
+        in_specs=[pl.BlockSpec(memory_space=pltpu.HBM)],
         out_specs=pl.BlockSpec(memory_space=pl.ANY),
         scratch_shapes=[
             *[pltpu.VMEM(places, bf)] * 2,
-            pltpu.VMEM((8, 512), bf),
             pltpu.VMEM((1024, 512), bf),
             *[pltpu.VMEM((2, B, 640), f4)] * 4,
             pltpu.VMEM((512, 512), f4),
             *[pltpu.VMEM((2, 512, 512), bf)] * 3,
             pltpu.VMEM((4, 512, 512), bf),
             pltpu.VMEM((512, 512), bf),
-            DMA, DMA((8,)), DMA, DMA((2, 2)), DMA((2, 2)), DMA, DMA,
+            DMA, DMA, DMA, DMA((2, 2)), DMA((2, 2)), DMA, DMA,
         ],
-        compiler_params=pltpu.CompilerParams(collective_id=0, has_side_effects=True, vmem_limit_bytes=56 * 2**20),
+        compiler_params=pltpu.CompilerParams(collective_id=0, has_side_effects=True, vmem_limit_bytes=24 * 2**20),
     )(momentum.reshape(places))
     update = update.reshape(weights.shape).astype(jnp.float32)
     return (shrink * weights.astype(jnp.float32) - step_rate * update).astype(jnp.bfloat16)

time: 104 us -> 89.8 us (0.86)
  Pallas kernels: 101 us -> 86.7 us
  other arithmetic: 2.58 us -> 1.36 us
  local copies, waits for them, and re-layouts: 0.01 us -> 1.23 us
    pallas_call x1, Pallas kernels: 101 us -> 86.7 us  [on_device(): pl.pallas_call(step_kernel, name='orthogonal_update', out_shape=jax.Shape...]
    convert_element_type x1, other arithmetic: 2.58 us -> 1.36 us  [on_device(): (shrink * weights.astype(jnp.float32) - step_rate * update).astype(jnp.bf...]
    unnamed x2 -> x4, local copies, waits for them, and re-layouts: 0.01 us -> 1.23 us
where the time goes in v4:
time: 89.8 us; the launch traced here: 89.3 us
  Pallas kernels  86.7 us (97%)
  other arithmetic  1.36 us (2%)
  local copies, waits for them, and re-layouts  1.23 us (1%)
    pallas_call x1, Pallas kernels, on_device(): pl.pallas_call(step_kernel, name='orthogonal_update', out_shape=jax.Shape...  86.7 us

profile of v4, /device:TPU:1, one launch (start us, length us, event | category | flops | bytes accessed | tf_op | source)
XLA Modules:
  0.0 89.3 jit_solution(9018519542904870567)
XLA Ops:
  0.0 0.0 copy-start
  0.0 1.2 %copy-done = bf16[1,128,8,512]{3,2,1,0:T(8,128)(2,1)S(1)} copy-done((bf16[1,128,8,512]{3,2,1,0:T(8,128)(2,1)S(1)}, bf16[1,128,8,512]{3,2,1,0:T(8,128)(2,1)}, u32[]{:S(2)}) %copy-start) | copy-done | bytes 1048600
  1.2 0.0 copy-start.1
  1.2 86.7 %orthogonal_update.1 = bf16[128,8,512]{2,1,0:T(8,128)(2,1)S(1)} custom-call(bf16[128,8,512]{2,1,0:T(8,128)(2,1)S(1)} %bitcast.5), custom_call_target="tpu_custom_call" | custom-call | tf_op jit(solution)/shard_map/orthogonal_update/pallas_call | solution.py:237
  87.9 0.0 copy-done.1
  88.0 1.4 %fusion = bf16[1,128,8,512]{3,2,1,0:T(8,128)(2,1)} fusion(bf16[128,8,512]{2,1,0:T(8,128)(2,1)S(1)} %orthogonal_update.1, bf16[1,128,8,512]{3,2,1,0:T(8,128)(2,1)S(1)} %copy-done.1), kind=kLoop, calls=%fused_computation.1 | loop fusion | flops 3145728 | bytes 3145728 | tf_op jit(solution)/shard_map/convert_element_type | solution.py:256
Async XLA Ops:
  0.0 1.2 %copy-start = (bf16[1,128,8,512]{3,2,1,0:T(8,128)(2,1)S(1)}, bf16[1,128,8,512]{3,2,1,0:T(8,128)(2,1)}, u32[]{:S(2)}) copy-start(bf16[1,128,8,512]{3,2,1,0:T(8,128)(2,1)} %param.2) | copy-start | bytes 3145732
  1.2 86.7 %copy-start.1 = (bf16[1,128,8,512]{3,2,1,0:T(8,128)(2,1)S(1)}, bf16[1,128,8,512]{3,2,1,0:T(8,128)(2,1)}, u32[]{:S(2)}) copy-start(bf16[1,128,8,512]{3,2,1,0:T(8,128)(2,1)} %param.3) | copy-start | bytes 3145732

commit v5 on v4

--- a/solution.py
+++ b/solution.py
@@ -70,18 +70,26 @@
 
     pltpu.make_async_copy(m_ref.at[opt], inb.at[opt], own).start()
 
+    columns = [ahead(z, turn) * 2 for turn in TURNS]
     barrier = pltpu.get_barrier_semaphore()
 
     def greet(k, carry):
-        pl.semaphore_signal(barrier, inc=1, device_id=(lax.rem(opt + k, 128), x), device_id_type=MESH)
-        return carry
-
-    lax.fori_loop(1, 128, greet, 0)
+        row = ahead(y, turn_of(k)) * 16
+        for place, column in enumerate(columns):
+            for core in range(2):
+                def signal(d=row + column + core):
+                    pl.semaphore_signal(barrier, inc=1, device_id=(d, x), device_id_type=MESH)
+
+                if place == 7:
+                    pl.when(row + column + core != opt)(signal)
+                else:
+                    signal()
+        return carry
+
+    lax.fori_loop(0, 8, greet, 0)
     for other in near:
         pl.semaphore_signal(barrier, inc=1, device_id=(opt, other), device_id_type=MESH)
     pl.semaphore_wait(barrier, 129)
-
-    columns = [ahead(z, turn) * 2 for turn in TURNS]
 
     def send(src, dst, sent, landed, d, place):
         def start():
@@ -122,22 +130,24 @@
     g[1, :, 384:640] = low[0:128]
     g[0, :, 512:640] = low[128:256, 128:]
 
-    def exchange(src, dst, stage, half):
-        other = near[(stage + half) % 2]
+    def exchange(src, dst, stage, part, half):
+        rows = pl.ds(part * 64, 64)
         return pltpu.make_async_remote_copy(
-            src.at[half], dst.at[half], x_send.at[stage, half], x_recv.at[stage, half],
-            device_id=(opt, other), device_id_type=MESH,
+            src.at[half, rows], dst.at[half, rows],
+            x_send.at[stage, half, part], x_recv.at[stage, half, part],
+            device_id=(opt, near[(stage + half) % 2]), device_id_type=MESH,
         )
 
-    for half in range(2):
-        exchange(g, ra, 0, half).start()
-
-    for half in range(2):
-        exchange(g, ra, 0, half).wait_recv()
-        g2[half] = g[half] + ra[half]
-        exchange(g2, rb, 1, half).start()
-    for half in range(2):
-        exchange(g2, rb, 1, half).wait_recv()
+    pieces = [(part, half) for part in range(2) for half in range(2)]
+    for piece in pieces:
+        exchange(g, ra, 0, *piece).start()
+    for part, half in pieces:
+        rows = pl.ds(part * 64, 64)
+        exchange(g, ra, 0, part, half).wait_recv()
+        g2[half, rows] = g[half, rows] + ra[half, rows]
+        exchange(g2, rb, 1, part, half).start()
+    for piece in pieces:
+        exchange(g2, rb, 1, *piece).wait_recv()
 
     where = {0: (0, 0), 1: (1, 0), 2: (1, 384), 3: (0, 512)}
 
@@ -208,9 +218,9 @@
 
     lax.fori_loop(0, 8, give_back, 0)
 
-    for half in range(2):
-        exchange(g, ra, 0, half).wait_send()
-        exchange(g2, rb, 1, half).wait_send()
+    for piece in pieces:
+        exchange(g, ra, 0, *piece).wait_send()
+        exchange(g2, rb, 1, *piece).wait_send()
     others = pl.ds(0, 127)
     pltpu.make_async_copy(inb.at[others], inb.at[others], in_send).wait()
     pltpu.make_async_copy(upd.at[others], upd.at[others], out_send).wait()
@@ -248,10 +258,10 @@
             *[pltpu.VMEM((2, 512, 512), bf)] * 3,
             pltpu.VMEM((4, 512, 512), bf),
             pltpu.VMEM((512, 512), bf),
-            DMA, DMA, DMA, DMA((2, 2)), DMA((2, 2)), DMA, DMA,
+            DMA, DMA, DMA, DMA((2, 2, 2)), DMA((2, 2, 2)), DMA, DMA,
         ],
         compiler_params=pltpu.CompilerParams(collective_id=0, has_side_effects=True, vmem_limit_bytes=24 * 2**20),
-    )(momentum.reshape(places))
+    )(pltpu.with_memory_space_constraint(momentum.reshape(places), pltpu.HBM))
     update = update.reshape(weights.shape).astype(jnp.float32)
     return (shrink * weights.astype(jnp.float32) - step_rate * update).astype(jnp.bfloat16)
 

time: 89.8 us -> 85.6 us (0.953)
  Pallas kernels: 86.7 us -> 84.1 us
  local copies, waits for them, and re-layouts: 1.23 us -> 0.01 us
    pallas_call x1, Pallas kernels: 86.7 us -> 84.1 us  [on_device(): pl.pallas_call(step_kernel, name='orthogonal_update', out_shape=jax.Shape...]
    unnamed x4 -> x2, local copies, waits for them, and re-layouts: 1.23 us -> 0.01 us
where the time goes in v5:
time: 85.6 us; the launch traced here: 85.5 us
  Pallas kernels  84.1 us (98%)
  other arithmetic  1.36 us (2%)
    pallas_call x1, Pallas kernels, on_device(): pl.pallas_call(step_kernel, name='orthogonal_update', out_shape=jax.Shape...  84.1 us

profile of v5, /device:TPU:1, one launch (start us, length us, event | category | flops | bytes accessed | tf_op | source)
XLA Modules:
  0.0 85.5 jit_solution(15774074327675047024)
XLA Ops:
  0.0 0.0 copy-start
  0.0 84.1 %orthogonal_update.1 = bf16[128,8,512]{2,1,0:T(8,128)(2,1)S(1)} custom-call(bf16[128,8,512]{2,1,0:T(8,128)(2,1)} %bitcast.5), custom_call_target="tpu_custom_call" | custom-call | tf_op jit(solution)/shard_map/orthogonal_update/pallas_call | solution.py:247
  84.1 0.0 copy-done
  84.1 1.4 %fusion = bf16[1,128,8,512]{3,2,1,0:T(8,128)(2,1)} fusion(bf16[128,8,512]{2,1,0:T(8,128)(2,1)S(1)} %orthogonal_update.1, bf16[1,128,8,512]{3,2,1,0:T(8,128)(2,1)S(1)} %copy-done), kind=kLoop, calls=%fused_computation.1 | loop fusion | flops 3145728 | bytes 3145728 | tf_op jit(solution)/shard_map/convert_element_type | solution.py:266
Async XLA Ops:
  0.0 84.1 %copy-start = (bf16[1,128,8,512]{3,2,1,0:T(8,128)(2,1)S(1)}, bf16[1,128,8,512]{3,2,1,0:T(8,128)(2,1)}, u32[]{:S(2)}) copy-start(bf16[1,128,8,512]{3,2,1,0:T(8,128)(2,1)} %param.3) | copy-start | bytes 3145732

commit v6 on v5

--- a/solution.py
+++ b/solution.py
@@ -210,8 +210,8 @@
     pltpu.make_async_copy(upd.at[opt], ub.at[opt], own).start()
 
     def give_back(k, carry):
-        row = ahead(y, turn_of(k)) * 16
         for place, column in enumerate(columns):
+            row = ahead(y, turn_of(lax.rem(k + place, 8))) * 16
             for core in range(2):
                 send(upd, ub, out_send, out_recv, row + column + core, place)
         return carry

time: 85.6 us -> 83.9 us (0.980)
  Pallas kernels: 84.1 us -> 82.4 us
    pallas_call x1, Pallas kernels: 84.1 us -> 82.4 us  [on_device(): pl.pallas_call(step_kernel, name='orthogonal_update', out_shape=jax.Shape...]
where the time goes in v6:
time: 83.9 us; the launch traced here: 83.8 us
  Pallas kernels  82.4 us (98%)
  other arithmetic  1.36 us (2%)
    pallas_call x1, Pallas kernels, on_device(): pl.pallas_call(step_kernel, name='orthogonal_update', out_shape=jax.Shape...  82.4 us

profile of v6, /device:TPU:1, one launch (start us, length us, event | category | flops | bytes accessed | tf_op | source)
XLA Modules:
  0.0 83.8 jit_solution(13216334356282406683)
XLA Ops:
  0.0 0.0 copy-start
  0.0 82.4 %orthogonal_update.1 = bf16[128,8,512]{2,1,0:T(8,128)(2,1)S(1)} custom-call(bf16[128,8,512]{2,1,0:T(8,128)(2,1)} %bitcast.5), custom_call_target="tpu_custom_call" | custom-call | tf_op jit(solution)/shard_map/orthogonal_update/pallas_call | solution.py:247
  82.4 0.0 copy-done
  82.4 1.4 %fusion = bf16[1,128,8,512]{3,2,1,0:T(8,128)(2,1)} fusion(bf16[128,8,512]{2,1,0:T(8,128)(2,1)S(1)} %orthogonal_update.1, bf16[1,128,8,512]{3,2,1,0:T(8,128)(2,1)S(1)} %copy-done), kind=kLoop, calls=%fused_computation.1 | loop fusion | flops 3145728 | bytes 3145728 | tf_op jit(solution)/shard_map/convert_element_type | solution.py:266
Async XLA Ops:
  0.0 82.4 %copy-start = (bf16[1,128,8,512]{3,2,1,0:T(8,128)(2,1)S(1)}, bf16[1,128,8,512]{3,2,1,0:T(8,128)(2,1)}, u32[]{:S(2)}) copy-start(bf16[1,128,8,512]{3,2,1,0:T(8,128)(2,1)} %param.3) | copy-start | bytes 3145732
